TPU v7x, 32 devices: a whole 2x2x4 slice. The times are simulated.
32 devices in a mesh: row: 8 (over y, x, core), col: 4 (over z).
Axes of the slice: x: 2, y: 2, z: 4, core: 2. Of those that a mesh axis runs over, the one named last changes fastest.
Arguments:
- coeffs: bfloat16 [16384, 2048], P('row', 'col'), may hold values from -0.8984375 to 0.8984375
- occupations: float32 [2048], replicated, may hold values from 0.05 to 2
- block_order: int32 [32], replicated, may hold values from 0 to 31, as said below
- neighbours: int32 [32, 15], P(('row', 'col')), may hold values from 0 to 31, as said below
- counts: int32 [32], P(('row', 'col')), may hold values from 4 to 15, as said below
Outputs:
- density: bfloat16 [32, 15, 512, 512], P(('row', 'col'))
Inputs may be any that keep to these rules, and one draw needn't show every extreme that they name: Within each aligned group of 4 entries, block_order is a permutation of that group's own indices. For atom row block a, the first counts[a] entries of neighbours[a] are distinct blocks b with |b - a| < 8; the remaining entries equal a. `counts`: some block has 15 live slots in every draw.
All inputs are finite; a program needn't handle non-finite values.
Results may differ from a plain program's by a relative error of at most 0.0044.
Values may be sent and summed in bfloat16 or wider, within the bound.
A program may use at most 128 MiB of HBM per device.

v0:
```python
import jax
import jax.numpy as jnp
from jax import lax
from jax.sharding import PartitionSpec as P

W = 8
NNB = 15


def from_behind(block, axis, distance):
    devices = range(lax.axis_size(axis))
    route = [(i - distance, i) for i in devices if i - distance in devices]
    return lax.ppermute(block, axis, route)


def shards(coeffs, occupations, block_order, neighbours, counts):
    col_count = lax.axis_size("col")
    states_local = coeffs.shape[1]
    block_rows = coeffs.shape[0] // col_count
    group_base = lax.axis_index("row") * col_count
    own_index = group_base + lax.axis_index("col")
    local_blocks = coeffs.reshape(col_count, block_rows, states_local)
    picks = lax.dynamic_slice_in_dim(block_order, group_base, col_count) - group_base
    outgoing = local_blocks[picks]
    own_block = lax.all_to_all(outgoing, "col", split_axis=0, concat_axis=2, tiled=True)
    downward = own_block
    step = 1
    while step < W:
        received = from_behind(downward, ("row", "col"), step)
        downward = jnp.concatenate([downward, received], axis=0)
        step = step * 2
    upward = own_block
    step = 1
    while step < W:
        received = from_behind(upward, ("row", "col"), -step)
        upward = jnp.concatenate([upward, received], axis=0)
        step = step * 2
    window = jnp.concatenate([downward[1:][::-1], upward], axis=0)
    weighted = (own_block[0].astype(jnp.float32) * occupations[None, :]).astype(jnp.bfloat16)
    offsets = neighbours[0] - own_index + (W - 1)
    live_count = counts[0]
    chosen = window[offsets]
    products = jnp.einsum("ik,jnk->jin", weighted, chosen, preferred_element_type=jnp.float32)
    slots = jnp.arange(NNB, dtype=jnp.int32)
    live = (slots < live_count)[:, None, None]
    result = jnp.where(live, products, 0.0).astype(jnp.bfloat16)
    return result[None]


def solution(mesh):
    return jax.shard_map(
        shards,
        mesh=mesh,
        in_specs=(P("row", "col"), P(), P(), P(("row", "col"), None), P(("row", "col"))),
        out_specs=P(("row", "col"), None, None, None),
        check_vma=False,
    )
```

profile of v0, /device:TPU:4, one launch (start us, length us, event | category | flops | bytes accessed | tf_op | source)
XLA Modules:
  0.0 819.4 jit_solution(5868224025195781986)
XLA Ops:
  0.0 0.9 compare_select_fusion.1
  0.9 0.7 copy-done
  1.6 2.0 gather_fusion
  3.6 53.1 %all_to_all.18 = bf16[4,512,512]{2,1,0:T(8,128)(2,1)S(1)} all-to-all(bf16[4,512,512]{2,1,0:T(8,128)(2,1)} %gather_fusion), channel_id=1, replica_groups=mesh['row'=8,'col'=4] {'col'}, dimensions={0} | all-to-all | bytes 4194304 | tf_op jit(solution)/shard_map/all_to_all | solution.py:25
  56.7 2.7 copy.19
  59.3 2.9 copy.20
  62.3 2.1 collective-permute-start
  64.4 7.0 collective-permute-start.3
  71.4 44.3 %collective-permute-done = bf16[1,512,2048]{2,1,0:T(8,128)(2,1)S(1)} collective-permute-done((bf16[1,512,2048]{2,1,0:T(8,128)(2,1)S(1)}, bf16[1,512,2048]{2,1,0:T(8,128)(2,1)S(1)}, u32[]{:S(2)}, u32[]{:S(2)}) %collective-permute-start) | collective-permute-done | bytes 2097184 | tf_op jit(solution)/shard_map/ppermute | solution.py:13
  115.7 41.6 %collective-permute-done.3 = bf16[1,512,2048]{2,1,0:T(8,128)(2,1)S(1)} collective-permute-done((bf16[1,512,2048]{2,1,0:T(8,128)(2,1)S(1)}, bf16[1,512,2048]{2,1,0:T(8,128)(2,1)S(1)}, u32[]{:S(2)}, u32[]{:S(2)}) %collective-permute-start.3) | collective-permute-done | bytes 2097184 | tf_op jit(solution)/shard_map/ppermute | solution.py:13
  158.0 1.9 collective-permute-start.1
  159.9 6.3 collective-permute-start.4
  166.3 268.8 %collective-permute-done.1 = bf16[2,512,2048]{2,1,0:T(8,128)(2,1)S(1)} collective-permute-done((bf16[2,512,2048]{2,1,0:T(8,128)(2,1)S(1)}, bf16[2,512,2048]{2,1,0:T(8,128)(2,1)S(1)}, u32[]{:S(2)}, u32[]{:S(2)}) %collective-permute-start.1) | collective-permute-done | bytes 4194336 | tf_op jit(solution)/shard_map/ppermute | solution.py:13
  435.0 86.1 %collective-permute-done.4 = bf16[2,512,2048]{2,1,0:T(8,128)(2,1)S(1)} collective-permute-done((bf16[2,512,2048]{2,1,0:T(8,128)(2,1)S(1)}, bf16[2,512,2048]{2,1,0:T(8,128)(2,1)S(1)}, u32[]{:S(2)}, u32[]{:S(2)}) %collective-permute-start.4) | collective-permute-done | bytes 4194336 | tf_op jit(solution)/shard_map/ppermute | solution.py:13
  521.1 6.8 fusion.7
  528.2 2.0 collective-permute-start.2
  530.3 4.9 collective-permute-start.5
  535.8 4.1 bitcast_convert_fusion
  540.0 5.3 copy.27
  545.3 4.0 fusion.11
  549.3 161.5 %collective-permute-done.2 = bf16[4,512,2048]{2,1,0:T(8,128)(2,1)} collective-permute-done((bf16[4,512,2048]{2,1,0:T(8,128)(2,1)}, bf16[4,512,2048]{2,1,0:T(8,128)(2,1)}, u32[]{:S(2)}, u32[]{:S(2)}) %collective-permute-start.2) | collective-permute-done | bytes 8388640 | tf_op jit(solution)/shard_map/ppermute | solution.py:13
  710.8 6.4 pad_maximum_fusion
  717.3 6.0 reverse_dynamic-update-slice_fusion
  723.3 1.6 constant_dynamic-update-slice_fusion.3
  724.8 1.5 constant_dynamic-update-slice_fusion.2
  727.0 2.3 constant_dynamic-update-slice_fusion.1
  729.3 8.4 %constant_dynamic-update-slice_fusion = bf16[15,512,2048]{2,1,0:T(8,128)(2,1)} fusion(bf16[15,512,2048]{2,1,0:T(8,128)(2,1)} %constant_dynamic-update-slice_fusion.1, bf16[4,512,2048]{2,1,0:T(8,128)(2,1)} %collective-permute-done.5), kind=kLoop, calls=%fused_computation.20 | loop fusion | bytes 16777216 | tf_op jit(solution)/shard_map/concatenate | solution.py:38
  737.7 23.1 %fusion.15 = (bf16[15,512,1024]{2,1,0:T(8,128)(2,1)}, bf16[15,512,1024]{2,1,0:T(8,128)(2,1)}) fusion(bf16[15,512,2048]{2,1,0:T(8,128)(2,1)} %constant_dynamic-update-slice_fusion), kind=kLoop, calls=%fused_computation.32 | loop fusion | bytes 62914560 | tf_op jit(solution)/shard_map/gather | solution.py:42
  760.8 12.4 %gather_fusion.1 = bf16[15,512,1024]{2,1,0:T(8,128)(2,1)} fusion(bf16[15,512,1024]{2,1,0:T(8,128)(2,1)} %get-tuple-element.5, s32[1024]{0:T(1024)S(1)} %pad_clamp_fusion), kind=kCustom, calls=%fused_computation.1 | custom fusion | bytes 31457340 | tf_op jit(solution)/shard_map/gather | solution.py:42
  773.2 12.5 %gather_fusion.2 = bf16[15,512,1024]{2,1,0:T(8,128)(2,1)} fusion(bf16[15,512,1024]{2,1,0:T(8,128)(2,1)} %get-tuple-element.6, s32[1024]{0:T(1024)S(1)} %pad_clamp_fusion), kind=kCustom, calls=%fused_computation.2 | custom fusion | bytes 31457340 | tf_op jit(solution)/shard_map/gather | solution.py:42
  785.7 23.1 %fusion.8 = bf16[1,15,512,512]{2,3,1,0:T(8,128)(2,1)} fusion(bf16[15,512,1024]{2,1,0:T(8,128)(2,1)} %gather_fusion.2, bf16[15,512,1024]{2,1,0:T(8,128)(2,1)} %gather_fusion.1, pred[15]{0:T(512)(128)(4,1)S(1)} %iota_compare_fusion, bf16[512,2048]{0,1:T(8,128)(2,1)} %fusion.11), kind=kOutput, calls=%fused_computation.14 | convolution fusion | flops 16176906240 | bytes 41418768 | tf_op jit(solution)/shard_map/ik,jnk->jin/dot_general | solution.py:43
  808.8 10.6 %copy.29 = bf16[1,15,512,512]{3,2,1,0:T(8,128)(2,1)} copy(bf16[1,15,512,512]{2,3,1,0:T(8,128)(2,1)} %fusion.8) | data formatting | bytes 15728640 | tf_op jit(solution)/shard_map/broadcast_in_dim | solution.py:47
  (29 shorter events, 1.7 us)
Async XLA Ops:
  0.0 1.6 copy-start
  56.7 2.7 copy-start.2
  62.3 53.4 %collective-permute-start = (bf16[1,512,2048]{2,1,0:T(8,128)(2,1)S(1)}, bf16[1,512,2048]{2,1,0:T(8,128)(2,1)S(1)}, u32[]{:S(2)}, u32[]{:S(2)}) collective-permute-start(bf16[1,512,2048]{2,1,0:T(8,128)(2,1)S(1)} %copy.20), channel_id=1, source_target_pairs={{0,1},{1,2},{2,3},{3,4},{4,5},{5,6},{6,7},{7,8},{8,9},{9,10},{10,1... | collective-permute-start | bytes 6291464 | tf_op jit(solution)/shard_map/ppermute | solution.py:13
  64.4 92.9 %collective-permute-start.3 = (bf16[1,512,2048]{2,1,0:T(8,128)(2,1)S(1)}, bf16[1,512,2048]{2,1,0:T(8,128)(2,1)S(1)}, u32[]{:S(2)}, u32[]{:S(2)}) collective-permute-start(bf16[1,512,2048]{2,1,0:T(8,128)(2,1)S(1)} %copy.20), channel_id=1, source_target_pairs={{1,0},{2,1},{3,2},{4,3},{5,4},{6,5},{7,6},{8,7},{9,8},{10,9},{11,1... | collective-permute-start | bytes 6291464 | tf_op jit(solution)/shard_map/ppermute | solution.py:13
  115.7 412.2 %copy-start.3 = (bf16[1,512,2048]{2,1,0:T(8,128)(2,1)}, bf16[1,512,2048]{2,1,0:T(8,128)(2,1)S(1)}, u32[]{:S(2)}) copy-start(bf16[1,512,2048]{2,1,0:T(8,128)(2,1)S(1)} %collective-permute-done) | copy-start | bytes 6291460
  157.3 370.6 %copy-start.4 = (bf16[1,512,2048]{2,1,0:T(8,128)(2,1)}, bf16[1,512,2048]{2,1,0:T(8,128)(2,1)S(1)}, u32[]{:S(2)}) copy-start(bf16[1,512,2048]{2,1,0:T(8,128)(2,1)S(1)} %collective-permute-done.3) | copy-start | bytes 6291460
  158.0 277.0 %collective-permute-start.1 = (bf16[2,512,2048]{2,1,0:T(8,128)(2,1)S(1)}, bf16[2,512,2048]{2,1,0:T(8,128)(2,1)S(1)}, u32[]{:S(2)}, u32[]{:S(2)}) collective-permute-start(bf16[2,512,2048]{2,1,0:T(8,128)(2,1)S(1)} %get-tuple-element.10), channel_id=1, source_target_pairs={{0,2},{1,3},{2,4},{3,5},{4,6},{5,7},{6,8},{7,9},{8,10},{9,11},{10,... | collective-permute-start | bytes 12582920 | tf_op jit(solution)/shard_map/ppermute | solution.py:13
  159.9 375.9 %copy-start.11 = (s32[1,15]{1,0:T(1,128)S(1)}, s32[1,15]{1,0:T(1,128)}, u32[]{:S(2)}) copy-start(s32[1,15]{1,0:T(1,128)} %param.8) | copy-start | bytes 184
  159.9 361.2 %collective-permute-start.4 = (bf16[2,512,2048]{2,1,0:T(8,128)(2,1)S(1)}, bf16[2,512,2048]{2,1,0:T(8,128)(2,1)S(1)}, u32[]{:S(2)}, u32[]{:S(2)}) collective-permute-start(bf16[2,512,2048]{2,1,0:T(8,128)(2,1)S(1)} %get-tuple-element.9), channel_id=1, source_target_pairs={{2,0},{3,1},{4,2},{5,3},{6,4},{7,5},{8,6},{9,7},{10,8},{11,9},{12,... | collective-permute-start | bytes 12582920 | tf_op jit(solution)/shard_map/ppermute | solution.py:13
  435.0 92.9 %copy-start.6 = (bf16[2,512,2048]{2,1,0:T(8,128)(2,1)}, bf16[2,512,2048]{2,1,0:T(8,128)(2,1)S(1)}, u32[]{:S(2)}) copy-start(bf16[2,512,2048]{2,1,0:T(8,128)(2,1)S(1)} %collective-permute-done.1) | copy-start | bytes 12582916
  521.1 7.1 copy-start.8
  528.2 17.0 %copy-start.10 = (f32[2048]{0:T(1024)S(1)}, f32[2048]{0:T(1024)}, u32[]{:S(2)}) copy-start(f32[2048]{0:T(1024)} %param.6) | copy-start | bytes 24580
  528.2 182.6 %collective-permute-start.2 = (bf16[4,512,2048]{2,1,0:T(8,128)(2,1)}, bf16[4,512,2048]{2,1,0:T(8,128)(2,1)}, u32[]{:S(2)}, u32[]{:S(2)}) collective-permute-start(bf16[4,512,2048]{2,1,0:T(8,128)(2,1)} %get-tuple-element.8), channel_id=1, source_target_pairs={{0,4},{1,5},{2,6},{3,7},{4,8},{5,9},{6,10},{7,11},{8,12},{9,13},{1... | collective-permute-start | bytes 25165832 | tf_op jit(solution)/shard_map/ppermute | solution.py:13
  530.3 199.0 %collective-permute-start.5 = (bf16[4,512,2048]{2,1,0:T(8,128)(2,1)}, bf16[4,512,2048]{2,1,0:T(8,128)(2,1)}, u32[]{:S(2)}, u32[]{:S(2)}) collective-permute-start(bf16[4,512,2048]{2,1,0:T(8,128)(2,1)} %get-tuple-element.7), channel_id=1, source_target_pairs={{4,0},{5,1},{6,2},{7,3},{8,4},{9,5},{10,6},{11,7},{12,8},{13,9},{1... | collective-permute-start | bytes 25165832 | tf_op jit(solution)/shard_map/ppermute | solution.py:13
  545.3 165.6 %copy-start.7 = (bf16[2,512,2048]{2,1,0:T(8,128)(2,1)S(1)}, bf16[2,512,2048]{2,1,0:T(8,128)(2,1)}, u32[]{:S(2)}) copy-start(bf16[2,512,2048]{2,1,0:T(8,128)(2,1)} %copy-done.6) | copy-start | bytes 12582916
  717.3 7.6 copy-start.5
  723.3 3.7 copy-start.9
  785.7 33.8 %copy-start.1 = (bf16[2048,512]{1,0:T(8,128)(2,1)S(1)}, bf16[2048,512]{1,0:T(8,128)(2,1)}, u32[]{:S(2)}) copy-start(bf16[2048,512]{1,0:T(8,128)(2,1)} %param.5) | copy-start | bytes 6291460
where the time goes:
time: 821 us; the launch traced here: 819 us
  waiting for transfers between devices  602 us (73%)
  local copies, waits for them, and re-layouts  92.9 us (11%)
  blocking collectives  53.1 us (6%)
  starting transfers between devices  24.3 us (3%)
  matrix products  23.1 us (3%)
  other arithmetic  22.9 us (3%)
    ppermute x6, waiting for transfers between devices, from_behind(): return lax.ppermute(block, axis, route)  602 us
    all_to_all x1, blocking collectives, shards(): lax.all_to_all(outgoing, 'col', split_axis=0, concat_axis=2, tiled=True)  53.1 us
    gather x3, local copies, waits for them, and re-layouts, shards(): chosen = window[offsets]  48 us
    ppermute x6, starting transfers between devices, from_behind(): return lax.ppermute(block, axis, route)  24.3 us
    dot_general x1, matrix products, shards(): jnp.einsum('ik,jnk->jin', weighted, chosen, preferred_element_type=jnp.fl...  23.1 us
  transfers between devices with their start and end apart: 6, of which 5 were waited for; matrix products, arithmetic and copies ran while one was open for 4% of the time, Pallas kernels for 0%

commit v1 on v0

--- a/solution.py
+++ b/solution.py
@@ -22,7 +22,10 @@
     local_blocks = coeffs.reshape(col_count, block_rows, states_local)
     picks = lax.dynamic_slice_in_dim(block_order, group_base, col_count) - group_base
     outgoing = local_blocks[picks]
-    own_block = lax.all_to_all(outgoing, "col", split_axis=0, concat_axis=2, tiled=True)
+    size = lax.axis_size("col")
+    blocks = jnp.stack(jnp.split(outgoing, size, axis=0), axis=0)
+    blocks = lax.all_to_all(blocks, "col", split_axis=0, concat_axis=0)
+    own_block = jnp.concatenate(blocks, axis=2)
     downward = own_block
     step = 1
     while step < W:

time: 821 us -> 822 us (level)
  no operation moved by 1% of the time
where the time goes in v1:
time: 822 us; the launch traced here: 821 us
  waiting for transfers between devices  602 us (73%)
  local copies, waits for them, and re-layouts  94.5 us (11%)
  blocking collectives  52.9 us (6%)
  starting transfers between devices  24.3 us (3%)
  other arithmetic  23.2 us (3%)
  matrix products  23.1 us (3%)
    ppermute x6, waiting for transfers between devices, from_behind(): return lax.ppermute(block, axis, route)  602 us
    all_to_all x1, blocking collectives, shards(): blocks = lax.all_to_all(blocks, 'col', split_axis=0, concat_axis=0)  52.9 us
    gather x3, local copies, waits for them, and re-layouts, shards(): chosen = window[offsets]  48 us
    ppermute x6, starting transfers between devices, from_behind(): return lax.ppermute(block, axis, route)  24.3 us
    dot_general x1, matrix products, shards(): jnp.einsum('ik,jnk->jin', weighted, chosen, preferred_element_type=jnp.fl...  23.1 us
  transfers between devices with their start and end apart: 6, of which 5 were waited for; matrix products, arithmetic and copies ran while one was open for 4% of the time, Pallas kernels for 0%

profile of v1, /device:TPU:4, one launch (start us, length us, event | category | flops | bytes accessed | tf_op | source)
XLA Modules:
  0.0 821.1 jit_solution(6784026010760056294)
XLA Ops:
  0.0 0.9 compare_select_fusion.1
  1.6 2.0 gather_fusion
  3.6 1.7 slice_bitcast_fusion.3
  5.5 52.9 %all_to_all.5 = bf16[4,1,512,512]{3,2,1,0:T(8,128)(2,1)S(1)} all-to-all(bf16[4,1,512,512]{3,2,1,0:T(8,128)(2,1)S(1)} %pad_maximum_fusion.5), channel_id=1, replica_groups=mesh['row'=8,'col'=4] {'col'}, dimensions={0} | all-to-all | bytes 4194304 | tf_op jit(solution)/shard_map/all_to_all | solution.py:27
  58.4 2.7 copy.22
  61.1 2.9 copy.23
  64.0 2.1 collective-permute-start
  66.1 7.0 collective-permute-start.3
  73.2 44.3 %collective-permute-done = bf16[1,512,2048]{2,1,0:T(8,128)(2,1)S(1)} collective-permute-done((bf16[1,512,2048]{2,1,0:T(8,128)(2,1)S(1)}, bf16[1,512,2048]{2,1,0:T(8,128)(2,1)S(1)}, u32[]{:S(2)}, u32[]{:S(2)}) %collective-permute-start) | collective-permute-done | bytes 2097184 | tf_op jit(solution)/shard_map/ppermute | solution.py:13
  117.4 41.6 %collective-permute-done.3 = bf16[1,512,2048]{2,1,0:T(8,128)(2,1)S(1)} collective-permute-done((bf16[1,512,2048]{2,1,0:T(8,128)(2,1)S(1)}, bf16[1,512,2048]{2,1,0:T(8,128)(2,1)S(1)}, u32[]{:S(2)}, u32[]{:S(2)}) %collective-permute-start.3) | collective-permute-done | bytes 2097184 | tf_op jit(solution)/shard_map/ppermute | solution.py:13
  159.7 1.9 collective-permute-start.1
  161.7 6.3 collective-permute-start.4
  168.0 268.8 %collective-permute-done.1 = bf16[2,512,2048]{2,1,0:T(8,128)(2,1)S(1)} collective-permute-done((bf16[2,512,2048]{2,1,0:T(8,128)(2,1)S(1)}, bf16[2,512,2048]{2,1,0:T(8,128)(2,1)S(1)}, u32[]{:S(2)}, u32[]{:S(2)}) %collective-permute-start.1) | collective-permute-done | bytes 4194336 | tf_op jit(solution)/shard_map/ppermute | solution.py:13
  436.8 86.1 %collective-permute-done.4 = bf16[2,512,2048]{2,1,0:T(8,128)(2,1)S(1)} collective-permute-done((bf16[2,512,2048]{2,1,0:T(8,128)(2,1)S(1)}, bf16[2,512,2048]{2,1,0:T(8,128)(2,1)S(1)}, u32[]{:S(2)}, u32[]{:S(2)}) %collective-permute-start.4) | collective-permute-done | bytes 4194336 | tf_op jit(solution)/shard_map/ppermute | solution.py:13
  522.9 6.8 fusion.7
  529.9 2.0 collective-permute-start.2
  532.0 4.9 collective-permute-start.5
  537.6 4.1 bitcast_convert_fusion
  541.7 5.3 copy.30
  547.0 4.0 fusion.11
  551.0 161.5 %collective-permute-done.2 = bf16[4,512,2048]{2,1,0:T(8,128)(2,1)} collective-permute-done((bf16[4,512,2048]{2,1,0:T(8,128)(2,1)}, bf16[4,512,2048]{2,1,0:T(8,128)(2,1)}, u32[]{:S(2)}, u32[]{:S(2)}) %collective-permute-start.2) | collective-permute-done | bytes 8388640 | tf_op jit(solution)/shard_map/ppermute | solution.py:13
  712.5 6.4 pad_maximum_fusion
  719.0 6.0 reverse_dynamic-update-slice_fusion
  725.0 1.6 constant_dynamic-update-slice_fusion.3
  726.5 1.5 constant_dynamic-update-slice_fusion.2
  728.7 2.3 constant_dynamic-update-slice_fusion.1
  731.0 8.4 %constant_dynamic-update-slice_fusion = bf16[15,512,2048]{2,1,0:T(8,128)(2,1)} fusion(bf16[15,512,2048]{2,1,0:T(8,128)(2,1)} %constant_dynamic-update-slice_fusion.1, bf16[4,512,2048]{2,1,0:T(8,128)(2,1)} %collective-permute-done.5), kind=kLoop, calls=%fused_computation.25 | loop fusion | bytes 16777216 | tf_op jit(solution)/shard_map/concatenate | solution.py:41
  739.4 23.1 %fusion.15 = (bf16[15,512,1024]{2,1,0:T(8,128)(2,1)}, bf16[15,512,1024]{2,1,0:T(8,128)(2,1)}) fusion(bf16[15,512,2048]{2,1,0:T(8,128)(2,1)} %constant_dynamic-update-slice_fusion), kind=kLoop, calls=%fused_computation.37 | loop fusion | bytes 62914560 | tf_op jit(solution)/shard_map/gather | solution.py:45
  762.5 12.4 %gather_fusion.1 = bf16[15,512,1024]{2,1,0:T(8,128)(2,1)} fusion(bf16[15,512,1024]{2,1,0:T(8,128)(2,1)} %get-tuple-element.5, s32[1024]{0:T(1024)S(1)} %pad_clamp_fusion), kind=kCustom, calls=%fused_computation.1 | custom fusion | bytes 31457340 | tf_op jit(solution)/shard_map/gather | solution.py:45
  774.9 12.5 %gather_fusion.2 = bf16[15,512,1024]{2,1,0:T(8,128)(2,1)} fusion(bf16[15,512,1024]{2,1,0:T(8,128)(2,1)} %get-tuple-element.6, s32[1024]{0:T(1024)S(1)} %pad_clamp_fusion), kind=kCustom, calls=%fused_computation.2 | custom fusion | bytes 31457340 | tf_op jit(solution)/shard_map/gather | solution.py:45
  787.4 23.1 %fusion.8 = bf16[1,15,512,512]{2,3,1,0:T(8,128)(2,1)} fusion(bf16[15,512,1024]{2,1,0:T(8,128)(2,1)} %gather_fusion.2, bf16[15,512,1024]{2,1,0:T(8,128)(2,1)} %gather_fusion.1, pred[15]{0:T(512)(128)(4,1)S(1)} %iota_compare_fusion, bf16[512,2048]{0,1:T(8,128)(2,1)} %fusion.11), kind=kOutput, calls=%fused_computation.14 | convolution fusion | flops 16176906240 | bytes 41418768 | tf_op jit(solution)/shard_map/ik,jnk->jin/dot_general | solution.py:46
  810.5 10.6 %copy.32 = bf16[1,15,512,512]{3,2,1,0:T(8,128)(2,1)} copy(bf16[1,15,512,512]{2,3,1,0:T(8,128)(2,1)} %fusion.8) | data formatting | bytes 15728640 | tf_op jit(solution)/shard_map/broadcast_in_dim | solution.py:50
  (31 shorter events, 2.6 us)
Async XLA Ops:
  0.0 1.6 copy-start
  58.4 2.7 copy-start.2
  64.0 53.4 %collective-permute-start = (bf16[1,512,2048]{2,1,0:T(8,128)(2,1)S(1)}, bf16[1,512,2048]{2,1,0:T(8,128)(2,1)S(1)}, u32[]{:S(2)}, u32[]{:S(2)}) collective-permute-start(bf16[1,512,2048]{2,1,0:T(8,128)(2,1)S(1)} %copy.23), channel_id=1, source_target_pairs={{0,1},{1,2},{2,3},{3,4},{4,5},{5,6},{6,7},{7,8},{8,9},{9,10},{10,1... | collective-permute-start | bytes 6291464 | tf_op jit(solution)/shard_map/ppermute | solution.py:13
  66.1 92.9 %collective-permute-start.3 = (bf16[1,512,2048]{2,1,0:T(8,128)(2,1)S(1)}, bf16[1,512,2048]{2,1,0:T(8,128)(2,1)S(1)}, u32[]{:S(2)}, u32[]{:S(2)}) collective-permute-start(bf16[1,512,2048]{2,1,0:T(8,128)(2,1)S(1)} %copy.23), channel_id=1, source_target_pairs={{1,0},{2,1},{3,2},{4,3},{5,4},{6,5},{7,6},{8,7},{9,8},{10,9},{11,1... | collective-permute-start | bytes 6291464 | tf_op jit(solution)/shard_map/ppermute | solution.py:13
  117.4 412.2 %copy-start.3 = (bf16[1,512,2048]{2,1,0:T(8,128)(2,1)}, bf16[1,512,2048]{2,1,0:T(8,128)(2,1)S(1)}, u32[]{:S(2)}) copy-start(bf16[1,512,2048]{2,1,0:T(8,128)(2,1)S(1)} %collective-permute-done) | copy-start | bytes 6291460
  159.1 370.6 %copy-start.4 = (bf16[1,512,2048]{2,1,0:T(8,128)(2,1)}, bf16[1,512,2048]{2,1,0:T(8,128)(2,1)S(1)}, u32[]{:S(2)}) copy-start(bf16[1,512,2048]{2,1,0:T(8,128)(2,1)S(1)} %collective-permute-done.3) | copy-start | bytes 6291460
  159.7 277.0 %collective-permute-start.1 = (bf16[2,512,2048]{2,1,0:T(8,128)(2,1)S(1)}, bf16[2,512,2048]{2,1,0:T(8,128)(2,1)S(1)}, u32[]{:S(2)}, u32[]{:S(2)}) collective-permute-start(bf16[2,512,2048]{2,1,0:T(8,128)(2,1)S(1)} %get-tuple-element.10), channel_id=1, source_target_pairs={{0,2},{1,3},{2,4},{3,5},{4,6},{5,7},{6,8},{7,9},{8,10},{9,11},{10,... | collective-permute-start | bytes 12582920 | tf_op jit(solution)/shard_map/ppermute | solution.py:13
  161.6 375.9 %copy-start.11 = (s32[1,15]{1,0:T(1,128)S(1)}, s32[1,15]{1,0:T(1,128)}, u32[]{:S(2)}) copy-start(s32[1,15]{1,0:T(1,128)} %param.8) | copy-start | bytes 184
  161.7 361.2 %collective-permute-start.4 = (bf16[2,512,2048]{2,1,0:T(8,128)(2,1)S(1)}, bf16[2,512,2048]{2,1,0:T(8,128)(2,1)S(1)}, u32[]{:S(2)}, u32[]{:S(2)}) collective-permute-start(bf16[2,512,2048]{2,1,0:T(8,128)(2,1)S(1)} %get-tuple-element.9), channel_id=1, source_target_pairs={{2,0},{3,1},{4,2},{5,3},{6,4},{7,5},{8,6},{9,7},{10,8},{11,9},{12,... | collective-permute-start | bytes 12582920 | tf_op jit(solution)/shard_map/ppermute | solution.py:13
  436.8 92.9 %copy-start.6 = (bf16[2,512,2048]{2,1,0:T(8,128)(2,1)}, bf16[2,512,2048]{2,1,0:T(8,128)(2,1)S(1)}, u32[]{:S(2)}) copy-start(bf16[2,512,2048]{2,1,0:T(8,128)(2,1)S(1)} %collective-permute-done.1) | copy-start | bytes 12582916
  522.9 7.1 copy-start.8
  529.9 17.0 %copy-start.10 = (f32[2048]{0:T(1024)S(1)}, f32[2048]{0:T(1024)}, u32[]{:S(2)}) copy-start(f32[2048]{0:T(1024)} %param.6) | copy-start | bytes 24580
  529.9 182.6 %collective-permute-start.2 = (bf16[4,512,2048]{2,1,0:T(8,128)(2,1)}, bf16[4,512,2048]{2,1,0:T(8,128)(2,1)}, u32[]{:S(2)}, u32[]{:S(2)}) collective-permute-start(bf16[4,512,2048]{2,1,0:T(8,128)(2,1)} %get-tuple-element.8), channel_id=1, source_target_pairs={{0,4},{1,5},{2,6},{3,7},{4,8},{5,9},{6,10},{7,11},{8,12},{9,13},{1... | collective-permute-start | bytes 25165832 | tf_op jit(solution)/shard_map/ppermute | solution.py:13
  532.0 199.0 %collective-permute-start.5 = (bf16[4,512,2048]{2,1,0:T(8,128)(2,1)}, bf16[4,512,2048]{2,1,0:T(8,128)(2,1)}, u32[]{:S(2)}, u32[]{:S(2)}) collective-permute-start(bf16[4,512,2048]{2,1,0:T(8,128)(2,1)} %get-tuple-element.7), channel_id=1, source_target_pairs={{4,0},{5,1},{6,2},{7,3},{8,4},{9,5},{10,6},{11,7},{12,8},{13,9},{1... | collective-permute-start | bytes 25165832 | tf_op jit(solution)/shard_map/ppermute | solution.py:13
  547.0 165.6 %copy-start.7 = (bf16[2,512,2048]{2,1,0:T(8,128)(2,1)S(1)}, bf16[2,512,2048]{2,1,0:T(8,128)(2,1)}, u32[]{:S(2)}) copy-start(bf16[2,512,2048]{2,1,0:T(8,128)(2,1)} %copy-done.6) | copy-start | bytes 12582916
  719.0 7.6 copy-start.5
  725.0 3.7 copy-start.9
  787.4 33.7 %copy-start.1 = (bf16[2048,512]{1,0:T(8,128)(2,1)S(1)}, bf16[2048,512]{1,0:T(8,128)(2,1)}, u32[]{:S(2)}) copy-start(bf16[2048,512]{1,0:T(8,128)(2,1)} %param.5) | copy-start | bytes 6291460
